TPU v7x, 256 devices: a whole 4x4x8 slice. The times are simulated.
256 devices in a mesh: dp: 32 (over y, z), vocab: 8 (over x, core).
Axes of the slice: x: 4, y: 4, z: 8, core: 2. Of those that a mesh axis runs over, the one named last changes fastest.
Arguments:
- hidden: bfloat16 [24576, 2048], P('dp', 'vocab')
- gain: bfloat16 [2048], replicated, may hold values from 0.5 to 1.5
- head: bfloat16 [2048, 32000], P('dp', 'vocab')
- target_ids: int32 [24576], P('dp'), may hold values from 0 to 31999
- seq_lens: int32 [64], replicated, may hold values from 64 to 704, as said below
- seq_owner: int32 [64], replicated, may hold values from 0 to 31, as said below
Outputs:
- logprob: float32 [24576], P('dp')
- entropy: float32 [24576], P('dp')
Inputs may be any that keep to these rules, and one draw needn't show every extreme that they name: `seq_lens`: the lengths of the sequences owned by one dp index sum to at most 768; in every draw the sequences of some dp index sum to exactly 768. `seq_owner`: every dp index owns exactly 2 sequences.
All inputs are finite; a program needn't handle non-finite values.
Results may differ from a plain program's by a relative error of at most 0.0075.
Values may be sent and summed in bfloat16 or wider, within the bound.
A program may use at most 64 MiB of HBM per device.

v0:
```python
import jax
import jax.numpy as jnp
from jax import lax
from jax.sharding import PartitionSpec as P

EPS = 1e-05


def chunk_bounds(breadth, parts):
    step = -(-breadth // parts)
    step = -(-step // 128) * 128
    bounds = []
    start = 0
    while start < breadth:
        stop = min(start + step, breadth)
        bounds.append((start, stop))
        start = stop
    return bounds


def chunk_stats(normed, columns, local_id, start):
    logits = jnp.dot(normed, columns, preferred_element_type=jnp.float32)
    top = jnp.max(logits, axis=1)
    expo = jnp.exp(logits - top[:, None])
    total = jnp.sum(expo, axis=1)
    weighted = jnp.sum(expo * logits, axis=1)
    ids = start + lax.broadcasted_iota(jnp.int32, logits.shape, 1)
    picked = jnp.sum(jnp.where(ids == local_id[:, None], logits, 0.0), axis=1)
    return (top, total, weighted, picked)


def local(hidden, gain, head, target_ids, seq_lens, seq_owner):
    groups = lax.axis_size("dp")
    position = lax.axis_index("dp")
    slice_index = lax.axis_index("vocab")
    slots = hidden.shape[0]
    breadth = head.shape[1]
    owners = jnp.arange(groups, dtype=jnp.int32)
    loads = jnp.sum(jnp.where(seq_owner[:, None] == owners[None, :], seq_lens[:, None], 0), axis=0)
    own_live = jnp.arange(slots, dtype=jnp.int32) < loads[position]
    features = lax.all_gather(hidden, "vocab", axis=1, tiled=True)
    wide = features.astype(jnp.float32)
    normed = (
        wide
        * lax.rsqrt(jnp.mean(wide * wide, axis=1, keepdims=True) + EPS)
        * gain.astype(jnp.float32)
    ).astype(jnp.bfloat16)
    local_id = target_ids - slice_index * breadth
    parts = []
    for start, stop in chunk_bounds(breadth, 4):
        columns = lax.all_gather(head[:, start:stop], "dp", axis=0, tiled=True)
        parts.append(chunk_stats(normed, columns, local_id, start))
    tops = jnp.stack([p[0] for p in parts])
    top_local = jnp.max(tops, axis=0)
    scale = jnp.exp(tops - top_local[None, :])
    total_local = jnp.sum(jnp.stack([p[1] for p in parts]) * scale, axis=0)
    weighted_local = jnp.sum(jnp.stack([p[2] for p in parts]) * scale, axis=0)
    picked_local = jnp.sum(jnp.stack([p[3] for p in parts]), axis=0)
    top = lax.pmax(top_local, "vocab")
    factor = jnp.exp(top_local - top)
    total, weighted, picked = lax.psum(
        (total_local * factor, weighted_local * factor, picked_local), "vocab"
    )
    lse = top + jnp.log(total)
    logprob = picked - lse
    entropy = lse - weighted / total
    return (jnp.where(own_live, logprob, 0.0), jnp.where(own_live, entropy, 0.0))


def solution(mesh):
    return jax.shard_map(
        local,
        mesh=mesh,
        in_specs=(P("dp", "vocab"), P(), P("dp", "vocab"), P("dp"), P(), P()),
        out_specs=(P("dp"), P("dp")),
        check_vma=False,
    )
```

profile of v0, /device:TPU:32, one launch (start us, length us, event | category | flops | bytes accessed | tf_op | source)
XLA Modules:
  0.0 432.0 jit_solution(7421292452426967437)
XLA Ops:
  7.2 0.0 all-gather.6.cloned.1.call-start
  7.2 0.7 all-gather.6.cloned.1.call-update
  7.9 0.0 all-gather.14.cloned.1.call-start
  7.9 1.6 slice.15
  9.5 0.0 all-gather.14.cloned.1.call-update
  9.5 0.0 all-gather.8.cloned.1.call-start
  9.6 1.8 fusion.20
  11.4 0.0 all-gather.8.cloned.1.call-update
  11.4 0.0 all-gather.10.cloned.1.call-start
  11.5 0.5 all-gather.10.cloned.1.call-update
  12.0 0.0 all-gather.12.cloned.1.call-start
  12.0 0.5 all-gather.12.cloned.1.call-update
  12.6 0.7 convert_element_type.10
  13.3 0.8 select_reduce_fusion.4
  14.1 0.7 dynamic_slice.3
  14.7 0.7 broadcast_subtract_fusion
  15.4 31.2 %all-gather.6.cloned.1.call-done = bf16[768,2048]{1,0:T(8,128)(2,1)} async-done(((bf16[768,256]{1,0:T(8,128)(2,1)}), bf16[768,2048]{1,0:T(8,128)(2,1)}) %all-gather.6.cloned.1.call-update) | async-done | bytes 3145744 | tf_op jit(solution)/shard_map/all_gather | solution.py:41
  46.6 0.0 copy-start.1
  46.6 2.7 fusion
  49.4 82.9 %all-gather.14.cloned.1.call-done = bf16[2048,928]{1,0:T(8,128)(2,1)} async-done(((bf16[64,928]{1,0:T(8,128)(2,1)}), bf16[2048,928]{1,0:T(8,128)(2,1)}) %all-gather.14.cloned.1.call-update) | async-done | bytes 3801104 | tf_op jit(solution)/shard_map/all_gather | solution.py:51
  132.3 0.0 copy-done.1
  132.3 5.9 %fusion.21 = (f32[768]{0:T(1024)S(1)}, f32[768,928]{0,1:T(8,128)S(1)}) fusion(bf16[2048,928]{1,0:T(8,128)(2,1)} %all-gather.14.cloned.1.call-done, bf16[768,2048]{1,0:T(8,128)(2,1)S(1)} %copy-done.1, f32[2048]{0:T(1024)S(1)} %convert_element_type.10, f32[768]{0:T(1024)S(1)} %add_rsqrt_fusion), kind=kOutput, calls=%fused_computation.49 | convolution fusion | flops 2926238976 | bytes 9811968 | tf_op jit(solution)/shard_map/dot_general | solution.py:22
  138.2 0.9 multiply_reduce_fusion.3
  139.0 74.9 %all-gather.8.cloned.1.call-done = bf16[2048,1024]{1,0:T(8,128)(2,1)} async-done(((bf16[64,1024]{1,0:T(8,128)(2,1)}), bf16[2048,1024]{1,0:T(8,128)(2,1)}) %all-gather.8.cloned.1.call-update) | async-done | bytes 4194320 | tf_op jit(solution)/shard_map/all_gather | solution.py:51
  214.0 6.4 %fusion.24 = (f32[768]{0:T(1024)S(1)}, f32[768,1024]{1,0:T(8,128)S(1)}) fusion(bf16[2048,1024]{1,0:T(8,128)(2,1)} %all-gather.8.cloned.1.call-done, bf16[768,2048]{1,0:T(8,128)(2,1)} %all-gather.6.cloned.1.call-done, f32[2048]{0:T(1024)S(1)} %convert_element_type.10, f32[768]{0:T(1024)S(1)} %add_rsqrt_fusion), kind=kOutput, calls=%fused_computation.52 | convolution fusion | flops 3228302592 | bytes 10500096 | tf_op jit(solution)/shard_map/dot_general | solution.py:22
  220.4 75.1 %all-gather.10.cloned.1.call-done = bf16[2048,1024]{1,0:T(8,128)(2,1)} async-done(((bf16[64,1024]{1,0:T(8,128)(2,1)}), bf16[2048,1024]{1,0:T(8,128)(2,1)}) %all-gather.10.cloned.1.call-update) | async-done | bytes 4194320 | tf_op jit(solution)/shard_map/all_gather | solution.py:51
  295.5 8.4 %fusion.22 = (f32[768]{0:T(1024)S(1)}, f32[768,1024]{1,0:T(8,128)}) fusion(bf16[2048,1024]{1,0:T(8,128)(2,1)} %all-gather.10.cloned.1.call-done, bf16[768,2048]{1,0:T(8,128)(2,1)} %all-gather.6.cloned.1.call-done, f32[2048]{0:T(1024)S(1)} %convert_element_type.10, f32[768]{0:T(1024)S(1)} %add_rsqrt_fusion), kind=kOutput, calls=%fused_computation.50 | convolution fusion | flops 3228302592 | bytes 10500096 | tf_op jit(solution)/shard_map/dot_general | solution.py:22
  303.8 73.2 %all-gather.12.cloned.1.call-done = bf16[2048,1024]{1,0:T(8,128)(2,1)} async-done(((bf16[64,1024]{1,0:T(8,128)(2,1)}), bf16[2048,1024]{1,0:T(8,128)(2,1)}) %all-gather.12.cloned.1.call-update) | async-done | bytes 4194320 | tf_op jit(solution)/shard_map/all_gather | solution.py:51
  377.0 0.0 copy-start
  377.0 6.6 %fusion.23 = (f32[768]{0:T(1024)S(1)}, f32[768,1024]{1,0:T(8,128)S(1)}) fusion(bf16[2048,1024]{1,0:T(8,128)(2,1)} %all-gather.12.cloned.1.call-done, bf16[768,2048]{1,0:T(8,128)(2,1)} %all-gather.6.cloned.1.call-done, f32[2048]{0:T(1024)S(1)} %convert_element_type.10, f32[768]{0:T(1024)S(1)} %add_rsqrt_fusion), kind=kOutput, calls=%fused_computation.51 | convolution fusion | flops 3228302592 | bytes 10500096 | tf_op jit(solution)/shard_map/dot_general | solution.py:22
  383.6 0.0 copy-done
  383.6 4.4 %multiply_reduce_fusion.1 = (f32[768]{0:T(1024)S(1)}, f32[768]{0:T(1024)S(1)}, f32[768]{0:T(1024)S(1)}, f32[768]{0:T(1024)S(1)}, f32[768]{0:T(1024)S(1)}, /*inde...) fusion(f32[768,1024]{1,0:T(8,128)S(1)} %copy-done, f32[768]{0:T(1024)S(1)} %get-tuple-element.34, ...), kind=kLoop, calls=%fused_computation.6 | loop fusion | flops 16508160 | bytes 9485312 | tf_op jit(solution)/shard_map/reduce_sum | solution.py:26
  388.1 12.4 %pmax.7 = f32[768]{0:T(1024)S(1)} all-reduce(f32[768]{0:T(1024)S(1)} %maximum_maximum_fusion), channel_id=1, replica_groups=mesh['dp'=32,'vocab'=8] {'vocab'}, use_global_device_ids=true, to_apply=%region_11.12 | all-reduce | flops 768 | bytes 6144 | tf_op jit(solution)/shard_map/pmax | solution.py:59
  400.5 0.1 fusion.9
  400.6 23.6 %all-reduce = (f32[768]{0:T(1024)S(1)}, f32[768]{0:T(1024)S(1)}, f32[768]{0:T(1024)S(1)}) all-reduce(f32[768]{0:T(1024)S(1)} %add_add_fusion, f32[768]{0:T(1024)S(1)} %get-tuple-element.25, f32[768]{0:T(1024)S(1)} %get-tuple-element.24), channel_id=1, replica_groups=mesh['dp'=32,'vocab'=8] {'vocab'}, use_global_device_ids=true, to_apply=%region_6.7 | all-reduce | flops 2304 | bytes 18432 | tf_op jit(solution)/shard_map/psum | solution.py:61
  424.2 1.3 subtract_select_fusion
  (18 shorter events, 0.1 us)
Async XLA Ops:
  7.2 39.5 %all-gather.6.cloned.1.call-start = ((), (), s32[]{:S(2)}) async-start(), calls=%async_computation | async-start | bytes 3538944 | tf_op jit(solution)/shard_map/all_gather | solution.py:41
  7.9 124.4 %all-gather.14.cloned.1.call-start = ((), (), s32[]{:S(2)}) async-start(), calls=%async_computation.4 | async-start | bytes 4325376 | tf_op jit(solution)/shard_map/all_gather | solution.py:51
  9.5 204.4 %all-gather.8.cloned.1.call-start = ((), (), s32[]{:S(2)}) async-start(), calls=%async_computation.1 | async-start | bytes 4325376 | tf_op jit(solution)/shard_map/all_gather | solution.py:51
  11.4 284.1 %all-gather.10.cloned.1.call-start = ((), (), s32[]{:S(2)}) async-start(), calls=%async_computation.2 | async-start | bytes 4325376 | tf_op jit(solution)/shard_map/all_gather | solution.py:51
  12.0 365.0 %all-gather.12.cloned.1.call-start = ((), (), s32[]{:S(2)}) async-start(), calls=%async_computation.3 | async-start | bytes 4325376 | tf_op jit(solution)/shard_map/all_gather | solution.py:51
  46.6 85.6 %copy-start.1 = (bf16[768,2048]{1,0:T(8,128)(2,1)S(1)}, bf16[768,2048]{1,0:T(8,128)(2,1)}, u32[]{:S(2)}) copy-start(bf16[768,2048]{1,0:T(8,128)(2,1)} %all-gather.6.cloned.1.call-done) | copy-start | bytes 9437188
  377.0 6.6 %copy-start = (f32[768,1024]{1,0:T(8,128)S(1)}, f32[768,1024]{1,0:T(8,128)}, u32[]{:S(2)}) copy-start(f32[768,1024]{1,0:T(8,128)} %get-tuple-element.35) | copy-start | bytes 9437188
Sparse Core Ops, SparseCore 0:
  9.8 36.7 all-gather.5
  49.2 83.0 all-gather.13
  134.9 79.0 all-gather.7
  216.4 79.0 all-gather.9
  297.9 79.0 all-gather.11
where the time goes:
time: 432 us
  waiting for transfers between devices  339 us (78%)
  blocking collectives  36 us (8%)
  matrix products  27.2 us (6%)
  between operations  13.9 us (3%)
  other arithmetic  11.6 us (3%)
    all_gather x4, waiting for transfers between devices, local(): columns = lax.all_gather(head[:, start:stop], 'dp', axis=0, tiled=True)  306 us
    all_gather x1, waiting for transfers between devices, local(): features = lax.all_gather(hidden, 'vocab', axis=1, tiled=True)  31.2 us
    dot_general x4, matrix products, chunk_stats(): logits = jnp.dot(normed, columns, preferred_element_type=jnp.float32)  27.2 us
    psum x1, blocking collectives, local(): lax.psum((total_local * factor, weighted_local * factor, picked_local), '...  23.6 us
    pmax x1, blocking collectives, local(): top = lax.pmax(top_local, 'vocab')  12.4 us
  transfers between devices with their start and end apart: 5, of which 5 were waited for; matrix products, arithmetic and copies ran while one was open for 7% of the time, Pallas kernels for 0%

commit v1 on v0

--- a/solution.py
+++ b/solution.py
@@ -38,7 +38,30 @@
     owners = jnp.arange(groups, dtype=jnp.int32)
     loads = jnp.sum(jnp.where(seq_owner[:, None] == owners[None, :], seq_lens[:, None], 0), axis=0)
     own_live = jnp.arange(slots, dtype=jnp.int32) < loads[position]
-    features = lax.all_gather(hidden, "vocab", axis=1, tiled=True)
+    z_new, r_now, current_block = (
+        jax.lax.axis_size("vocab"),
+        jax.lax.axis_index("vocab"),
+        hidden.shape[1],
+    )
+    all_blocks = [j0 * z_new if num == 1 else j0 for num, j0 in enumerate(hidden.shape)]
+    features = lax.dynamic_update_slice_in_dim(
+        jnp.zeros(all_blocks, hidden.dtype), hidden, r_now * current_block, axis=1
+    )
+    value_now = clean = hidden
+    for idx in range(1, z_new // 2 + 1):
+        value_now = jax.lax.ppermute(
+            value_now, axis_name="vocab", perm=[(num, (num + 1) % z_new) for num in range(z_new)]
+        )
+        features = lax.dynamic_update_slice_in_dim(
+            features, value_now, (r_now - idx) % z_new * current_block, axis=1
+        )
+        if 2 * idx < z_new:
+            clean = jax.lax.ppermute(
+                clean, axis_name="vocab", perm=[(num, (num - 1) % z_new) for num in range(z_new)]
+            )
+            features = lax.dynamic_update_slice_in_dim(
+                features, clean, (r_now + idx) % z_new * current_block, axis=1
+            )
     wide = features.astype(jnp.float32)
     normed = (
         wide

time: 432 us -> 395 us (0.914)
  waiting for transfers between devices: 339 us -> 290 us
  starting transfers between devices: 0.2 us -> 9 us
  local copies, waits for them, and re-layouts: 4.11 us -> 9.39 us
    all_gather x4, waiting for transfers between devices: 306 us -> 271 us  [local(): columns = lax.all_gather(head[:, start:stop], 'dp', axis=0, tiled=True)]
    all_gather x1 -> x0, waiting for transfers between devices: 31.2 us -> none  [local(): features = lax.all_gather(hidden, 'vocab', axis=1, tiled=True)]
    ppermute x0 -> x7, waiting for transfers between devices: none -> 16.9 us  [the longest x4 16.9 us: local(): jax.lax.ppermute(value_now, axis_name='vocab', perm=[(num, (num + 1) % z_...]
    ppermute x0 -> x7, starting transfers between devices: none -> 8.84 us  [the longest x3 8.81 us: local(): jax.lax.ppermute(clean, axis_name='vocab', perm=[(num, (num - 1) % z_new)...]
    dynamic_update_slice x0 -> x8, local copies, waits for them, and re-layouts: none -> 4.35 us  [the longest x4 2.17 us: local(): lax.dynamic_update_slice_in_dim(features, value_now, (r_now - idx) % z_ne...]
  transfers between devices with their start and end apart: 5 -> 11, of which waited for: 5 -> 8; matrix products, arithmetic and copies ran while one was open for 7% -> 8% of each run, Pallas kernels for 0% -> 0%
where the time goes in v1:
time: 395 us; the launch traced here: 394 us
  waiting for transfers between devices  290 us (73%)
  blocking collectives  36 us (9%)
  matrix products  26.1 us (7%)
  between operations  14 us (4%)
  other arithmetic  10.1 us (3%)
  local copies, waits for them, and re-layouts  9.39 us (2%)
  starting transfers between devices  9 us (2%)
    all_gather x4, waiting for transfers between devices, local(): columns = lax.all_gather(head[:, start:stop], 'dp', axis=0, tiled=True)  271 us
    dot_general x4, matrix products, chunk_stats(): logits = jnp.dot(normed, columns, preferred_element_type=jnp.float32)  26.1 us
    psum x1, blocking collectives, local(): lax.psum((total_local * factor, weighted_local * factor, picked_local), '...  23.6 us
    ppermute x4, waiting for transfers between devices, local(): jax.lax.ppermute(value_now, axis_name='vocab', perm=[(num, (num + 1) % z_...  16.9 us
    pmax x1, blocking collectives, local(): top = lax.pmax(top_local, 'vocab')  12.4 us
    ppermute x3, starting transfers between devices, local(): jax.lax.ppermute(clean, axis_name='vocab', perm=[(num, (num - 1) % z_new)...  8.81 us
  transfers between devices with their start and end apart: 11, of which 8 were waited for; matrix products, arithmetic and copies ran while one was open for 8% of the time, Pallas kernels for 0%

profile of v1, /device:TPU:32, one launch (start us, length us, event | category | flops | bytes accessed | tf_op | source)
XLA Modules:
  0.0 394.1 jit_solution(15786374608068407700)
XLA Ops:
  7.2 0.0 copy-start.2
  7.2 0.0 all-gather.11.cloned.1.call-start
  7.2 1.6 slice.15
  8.8 0.0 all-gather.11.cloned.1.call-update
  8.8 0.0 all-gather.9.cloned.1.call-start
  8.9 1.8 fusion.20
  10.7 0.0 all-gather.9.cloned.1.call-update
  10.7 0.0 all-gather.7.cloned.1.call-start
  10.8 0.7 all-gather.7.cloned.1.call-update
  11.5 0.0 all-gather.5.cloned.1.call-start
  11.5 0.5 all-gather.5.cloned.1.call-update
  12.0 0.0 collective-permute-start
  12.1 2.9 collective-permute-start.1
  15.0 5.7 %collective-permute-done = bf16[768,256]{1,0:T(8,128)(2,1)S(1)} collective-permute-done((bf16[768,256]{1,0:T(8,128)(2,1)}, bf16[768,256]{1,0:T(8,128)(2,1)S(1)}, u32[]{:S(2)}, u32[]{:S(2)}) %collective-permute-start) | collective-permute-done | bytes 393248 | tf_op jit(solution)/shard_map/ppermute | solution.py:52
  20.7 0.0 collective-permute-start.2
  20.7 0.8 select_reduce_fusion.4
  21.5 0.7 broadcast_subtract_fusion
  22.2 0.0 collective-permute-done.1
  22.2 2.9 collective-permute-start.3
  25.1 4.1 %collective-permute-done.2 = bf16[768,256]{1,0:T(8,128)(2,1)} collective-permute-done((bf16[768,256]{1,0:T(8,128)(2,1)S(1)}, bf16[768,256]{1,0:T(8,128)(2,1)}, u32[]{:S(2)}, u32[]{:S(2)}) %collective-permute-start.2) | collective-permute-done | bytes 393248 | tf_op jit(solution)/shard_map/ppermute | solution.py:52
  29.2 0.0 collective-permute-start.4
  29.2 1.3 convert_element_type.10
  30.5 0.6 dynamic_slice.3
  31.1 0.4 broadcast_in_dim.46
  31.6 0.5 copy-done.4
  32.2 0.0 collective-permute-done.3
  32.2 3.0 collective-permute-start.5
  35.1 1.0 constant_dynamic-update-slice_fusion.4
  36.2 1.7 collective-permute-done.4
  37.9 1.0 constant_dynamic-update-slice_fusion.3
  39.0 1.0 constant_dynamic-update-slice_fusion.2
  40.0 1.1 constant_dynamic-update-slice_fusion.1
  41.2 5.4 %collective-permute-done.6 = bf16[768,256]{1,0:T(8,128)(2,1)S(1)} collective-permute-done((bf16[768,256]{1,0:T(8,128)(2,1)}, bf16[768,256]{1,0:T(8,128)(2,1)S(1)}, u32[]{:S(2)}, u32[]{:S(2)}) %collective-permute-start.6) | collective-permute-done | bytes 393248 | tf_op jit(solution)/shard_map/ppermute | solution.py:52
  46.6 0.7 fusion
  47.3 47.9 %all-gather.11.cloned.1.call-done = bf16[2048,928]{1,0:T(8,128)(2,1)} async-done(((bf16[64,928]{1,0:T(8,128)(2,1)}), bf16[2048,928]{1,0:T(8,128)(2,1)}) %all-gather.11.cloned.1.call-update) | async-done | bytes 3801104 | tf_op jit(solution)/shard_map/all_gather | solution.py:74
  95.2 5.7 %fusion.21 = (f32[768]{0:T(1024)S(1)}, f32[768,928]{0,1:T(8,128)S(1)}) fusion(bf16[2048,928]{1,0:T(8,128)(2,1)} %all-gather.11.cloned.1.call-done, bf16[768,2048]{1,0:T(8,128)(2,1)S(1)} %constant_dynamic-update-slice_fusion.7, f32[2048]{0:T(1024)S(1)} %copy-done.5, f32[768]{0:T(1024)S(1)} %add_rsqrt_fusion), kind=kOutput, calls=%fused_computation.57 | convolution fusion | flops 2926238976 | bytes 9811968 | tf_op jit(solution)/shard_map/dot_general | solution.py:22
  101.0 0.9 multiply_reduce_fusion.3
  101.9 75.1 %all-gather.9.cloned.1.call-done = bf16[2048,1024]{1,0:T(8,128)(2,1)} async-done(((bf16[64,1024]{1,0:T(8,128)(2,1)}), bf16[2048,1024]{1,0:T(8,128)(2,1)}) %all-gather.9.cloned.1.call-update) | async-done | bytes 4194320 | tf_op jit(solution)/shard_map/all_gather | solution.py:74
  176.9 7.4 %fusion.23 = (f32[768]{0:T(1024)S(1)}, f32[768,1024]{1,0:T(8,128)}) fusion(bf16[2048,1024]{1,0:T(8,128)(2,1)} %all-gather.9.cloned.1.call-done, bf16[768,2048]{1,0:T(8,128)(2,1)S(1)} %constant_dynamic-update-slice_fusion.7, f32[2048]{0:T(1024)S(1)} %copy-done.5, f32[768]{0:T(1024)S(1)} %add_rsqrt_fusion), kind=kOutput, calls=%fused_computation.59 | convolution fusion | flops 3228302592 | bytes 10500096 | tf_op jit(solution)/shard_map/dot_general | solution.py:22
  184.3 74.3 %all-gather.7.cloned.1.call-done = bf16[2048,1024]{1,0:T(8,128)(2,1)} async-done(((bf16[64,1024]{1,0:T(8,128)(2,1)}), bf16[2048,1024]{1,0:T(8,128)(2,1)}) %all-gather.7.cloned.1.call-update) | async-done | bytes 4194320 | tf_op jit(solution)/shard_map/all_gather | solution.py:74
  258.6 7.4 %fusion.22 = (f32[768]{0:T(1024)S(1)}, f32[768,1024]{1,0:T(8,128)}) fusion(bf16[2048,1024]{1,0:T(8,128)(2,1)} %all-gather.7.cloned.1.call-done, bf16[768,2048]{1,0:T(8,128)(2,1)S(1)} %constant_dynamic-update-slice_fusion.7, f32[2048]{0:T(1024)S(1)} %copy-done.5, f32[768]{0:T(1024)S(1)} %add_rsqrt_fusion), kind=kOutput, calls=%fused_computation.58 | convolution fusion | flops 3228302592 | bytes 10500096 | tf_op jit(solution)/shard_map/dot_general | solution.py:22
  266.0 74.1 %all-gather.5.cloned.1.call-done = bf16[2048,1024]{1,0:T(8,128)(2,1)} async-done(((bf16[64,1024]{1,0:T(8,128)(2,1)}), bf16[2048,1024]{1,0:T(8,128)(2,1)}) %all-gather.5.cloned.1.call-update) | async-done | bytes 4194320 | tf_op jit(solution)/shard_map/all_gather | solution.py:74
  340.1 5.6 %fusion.24 = (f32[768]{0:T(1024)S(1)}, f32[768,1024]{1,0:T(8,128)S(1)}) fusion(bf16[2048,1024]{1,0:T(8,128)(2,1)} %all-gather.5.cloned.1.call-done, bf16[768,2048]{1,0:T(8,128)(2,1)S(1)} %constant_dynamic-update-slice_fusion.7, f32[2048]{0:T(1024)S(1)} %copy-done.5, f32[768]{0:T(1024)S(1)} %add_rsqrt_fusion), kind=kOutput, calls=%fused_computation.60 | convolution fusion | flops 3228302592 | bytes 10500096 | tf_op jit(solution)/shard_map/dot_general | solution.py:22
  345.8 4.4 %multiply_reduce_fusion.1 = (f32[768]{0:T(1024)S(1)}, f32[768]{0:T(1024)S(1)}, f32[768]{0:T(1024)S(1)}, f32[768]{0:T(1024)S(1)}, f32[768]{0:T(1024)S(1)}, /*inde...) fusion(f32[768,1024]{1,0:T(8,128)S(1)} %copy-done.1, f32[768]{0:T(1024)S(1)} %get-tuple-element.34, ...), kind=kLoop, calls=%fused_computation.6 | loop fusion | flops 16508160 | bytes 9485312 | tf_op jit(solution)/shard_map/reduce_sum | solution.py:26
  350.2 12.4 %pmax.7 = f32[768]{0:T(1024)S(1)} all-reduce(f32[768]{0:T(1024)S(1)} %maximum_maximum_fusion), channel_id=1, replica_groups=mesh['dp'=32,'vocab'=8] {'vocab'}, use_global_device_ids=true, to_apply=%region_11.12 | all-reduce | flops 768 | bytes 6144 | tf_op jit(solution)/shard_map/pmax | solution.py:82
  362.7 0.1 fusion.9
  362.8 23.6 %all-reduce = (f32[768]{0:T(1024)S(1)}, f32[768]{0:T(1024)S(1)}, f32[768]{0:T(1024)S(1)}) all-reduce(f32[768]{0:T(1024)S(1)} %add_add_fusion, f32[768]{0:T(1024)S(1)} %get-tuple-element.25, f32[768]{0:T(1024)S(1)} %get-tuple-element.24), channel_id=1, replica_groups=mesh['dp'=32,'vocab'=8] {'vocab'}, use_global_device_ids=true, to_apply=%region_6.7 | all-reduce | flops 2304 | bytes 18432 | tf_op jit(solution)/shard_map/psum | solution.py:84
  386.3 1.2 subtract_select_fusion
  (34 shorter events, 0.3 us)
Async XLA Ops:
  7.2 24.4 %copy-start.2 = (bf16[768,256]{1,0:T(8,128)(2,1)S(1)}, bf16[768,256]{1,0:T(8,128)(2,1)}, u32[]{:S(2)}) copy-start(bf16[768,256]{1,0:T(8,128)(2,1)} %param.6) | copy-start | bytes 1179652
  7.2 88.1 %all-gather.11.cloned.1.call-start = ((), (), s32[]{:S(2)}) async-start(), calls=%async_computation.3 | async-start | bytes 4325376 | tf_op jit(solution)/shard_map/all_gather | solution.py:74
  8.8 168.1 %all-gather.9.cloned.1.call-start = ((), (), s32[]{:S(2)}) async-start(), calls=%async_computation.2 | async-start | bytes 4325376 | tf_op jit(solution)/shard_map/all_gather | solution.py:74
  10.7 247.9 %all-gather.7.cloned.1.call-start = ((), (), s32[]{:S(2)}) async-start(), calls=%async_computation.1 | async-start | bytes 4325376 | tf_op jit(solution)/shard_map/all_gather | solution.py:74
  11.5 328.7 %all-gather.5.cloned.1.call-start = ((), (), s32[]{:S(2)}) async-start(), calls=%async_computation | async-start | bytes 4325376 | tf_op jit(solution)/shard_map/all_gather | solution.py:74
  12.0 8.6 %collective-permute-start = (bf16[768,256]{1,0:T(8,128)(2,1)}, bf16[768,256]{1,0:T(8,128)(2,1)S(1)}, u32[]{:S(2)}, u32[]{:S(2)}) collective-permute-start(bf16[768,256]{1,0:T(8,128)(2,1)} %param.6), channel_id=1, source_target_pairs={{0,1},{1,2},{2,3},{3,4},{4,5},{5,6},{6,7},{7,0},{8,9},{9,10},{10,1... | collective-permute-start | bytes 1179656 | tf_op jit(solution)/shard_map/ppermute | solution.py:52
  12.1 10.1 %collective-permute-start.1 = (bf16[768,256]{1,0:T(8,128)(2,1)}, bf16[768,256]{1,0:T(8,128)(2,1)}, u32[]{:S(2)}, u32[]{:S(2)}) collective-permute-start(bf16[768,256]{1,0:T(8,128)(2,1)} %param.6), channel_id=1, source_target_pairs={{0,7},{1,0},{2,1},{3,2},{4,3},{5,4},{6,5},{7,6},{8,15},{9,8},{10,9... | collective-permute-start | bytes 1179656 | tf_op jit(solution)/shard_map/ppermute | solution.py:59
  20.7 9.8 %copy-start.3 = (bf16[768,256]{1,0:T(8,128)(2,1)}, bf16[768,256]{1,0:T(8,128)(2,1)S(1)}, u32[]{:S(2)}) copy-start(bf16[768,256]{1,0:T(8,128)(2,1)S(1)} %collective-permute-done) | copy-start | bytes 1179652
  20.7 8.5 %collective-permute-start.2 = (bf16[768,256]{1,0:T(8,128)(2,1)S(1)}, bf16[768,256]{1,0:T(8,128)(2,1)}, u32[]{:S(2)}, u32[]{:S(2)}) collective-permute-start(bf16[768,256]{1,0:T(8,128)(2,1)S(1)} %collective-permute-done), channel_id=1, source_target_pairs={{0,1},{1,2},{2,3},{3,4},{4,5},{5,6},{6,7},{7,0},{8,9},{9,10},{10,1... | collective-permute-start | bytes 1179656 | tf_op jit(solution)/shard_map/ppermute | solution.py:52
  22.2 10.0 %collective-permute-start.3 = (bf16[768,256]{1,0:T(8,128)(2,1)}, bf16[768,256]{1,0:T(8,128)(2,1)}, u32[]{:S(2)}, u32[]{:S(2)}) collective-permute-start(bf16[768,256]{1,0:T(8,128)(2,1)} %collective-permute-done.1), channel_id=1, source_target_pairs={{0,7},{1,0},{2,1},{3,2},{4,3},{5,4},{6,5},{7,6},{8,15},{9,8},{10,9... | collective-permute-start | bytes 1179656 | tf_op jit(solution)/shard_map/ppermute | solution.py:59
  29.2 8.7 %collective-permute-start.4 = (bf16[768,256]{1,0:T(8,128)(2,1)}, bf16[768,256]{1,0:T(8,128)(2,1)}, u32[]{:S(2)}, u32[]{:S(2)}) collective-permute-start(bf16[768,256]{1,0:T(8,128)(2,1)} %collective-permute-done.2), channel_id=1, source_target_pairs={{0,1},{1,2},{2,3},{3,4},{4,5},{5,6},{6,7},{7,0},{8,9},{9,10},{10,1... | collective-permute-start | bytes 1179656 | tf_op jit(solution)/shard_map/ppermute | solution.py:52
  31.1 1.0 copy-start.4
  32.2 8.9 %collective-permute-start.5 = (bf16[768,256]{1,0:T(8,128)(2,1)}, bf16[768,256]{1,0:T(8,128)(2,1)S(1)}, u32[]{:S(2)}, u32[]{:S(2)}) collective-permute-start(bf16[768,256]{1,0:T(8,128)(2,1)} %collective-permute-done.3), channel_id=1, source_target_pairs={{0,7},{1,0},{2,1},{3,2},{4,3},{5,4},{6,5},{7,6},{8,15},{9,8},{10,9... | collective-permute-start | bytes 1179656 | tf_op jit(solution)/shard_map/ppermute | solution.py:59
  37.9 8.6 %collective-permute-start.6 = (bf16[768,256]{1,0:T(8,128)(2,1)}, bf16[768,256]{1,0:T(8,128)(2,1)S(1)}, u32[]{:S(2)}, u32[]{:S(2)}) collective-permute-start(bf16[768,256]{1,0:T(8,128)(2,1)} %collective-permute-done.4), channel_id=1, source_target_pairs={{0,1},{1,2},{2,3},{3,4},{4,5},{5,6},{6,7},{7,0},{8,9},{9,10},{10,1... | collective-permute-start | bytes 1179656 | tf_op jit(solution)/shard_map/ppermute | solution.py:52
  39.0 56.3 %copy-start.5 = (f32[2048]{0:T(1024)S(1)}, f32[2048]{0:T(1024)}, u32[]{:S(2)}) copy-start(f32[2048]{0:T(1024)} %convert_element_type.10) | copy-start | bytes 24580
  340.1 5.6 %copy-start = (f32[768,1024]{1,0:T(8,128)S(1)}, f32[768,1024]{1,0:T(8,128)}, u32[]{:S(2)}) copy-start(f32[768,1024]{1,0:T(8,128)} %get-tuple-element.37) | copy-start | bytes 9437188
  340.1 5.6 %copy-start.1 = (f32[768,1024]{1,0:T(8,128)S(1)}, f32[768,1024]{1,0:T(8,128)}, u32[]{:S(2)}) copy-start(f32[768,1024]{1,0:T(8,128)} %get-tuple-element.35) | copy-start | bytes 9437188
Sparse Core Ops, SparseCore 0:
  10.6 84.5 all-gather.10
  97.8 79.0 all-gather.8
  179.5 79.0 all-gather.6
  261.0 79.0 all-gather.4
